TPU v7x, 32 devices: a whole 2x2x4 slice. The times are simulated.
32 devices in a mesh: head: 4 (over y, x), batch: 8 (over z, core).
Axes of the slice: x: 2, y: 2, z: 4, core: 2. Of those that a mesh axis runs over, the one named last changes fastest.
Arguments:
- hidden_in: bfloat16 [8, 256, 4096], P('batch', None, 'head')
- w_query: bfloat16 [4096, 4096], P('batch', 'head'), may hold values from -0.09375 to 0.09375
- w_key: bfloat16 [4096, 4096], P('batch', 'head'), may hold values from -0.09375 to 0.09375
- w_value: bfloat16 [4096, 4096], P('batch', 'head'), may hold values from -0.09375 to 0.09375
- w_beta: bfloat16 [4096, 32], P('batch', 'head'), may hold values from -0.09375 to 0.09375
- w_out: bfloat16 [4096, 4096], P('head', 'batch'), may hold values from -0.125 to 0.125
- mem_pos: int32 [8, 2, 64], P('batch'), may hold values from 0 to 127, as said below
- memory_in: float32 [8, 32, 128, 128], P('batch', 'head'), may hold values from -6 to 6
Outputs:
- hidden_out: bfloat16 [8, 256, 4096], P('batch', None, 'head')
- memory_out: float32 [8, 32, 128, 128], P('batch', 'head')
Inputs may be any that keep to these rules, and one draw needn't show every extreme that they name: `mem_pos`: within each sequence and segment the 64 positions are distinct and ascending.
All inputs are finite; a program needn't handle non-finite values.
Results may differ from a plain program's by a relative error of at most 0.005.
Values may be sent and summed in bfloat16 or wider, within the bound.
No kernel may reach another device: no remote copies, remote signals or barrier semaphores. Data moves between devices by JAX's collectives and lax.ppermute only.
A program may use at most 128 MiB of HBM per device.

v0:
```python
import jax
import jax.numpy as jnp
from jax import lax
from jax.sharding import PartitionSpec as P

SEGS = 2
epsilon = 1e-05


def recur(query, keys, values, beta, state):
    highest = lax.Precision.HIGHEST
    readouts = []
    for segment in range(query.shape[1]):
        readouts.append(
            jnp.einsum("bhij,blhj->blhi", state, query[:, segment], precision=highest).astype(
                jnp.bfloat16
            )
        )
        recalled = jnp.einsum("bhij,bmhj->bmhi", state, keys[:, segment], precision=highest)
        change = beta[:, segment][..., None] * (values[:, segment] - recalled)
        state = state + jnp.einsum("bmhi,bmhj->bhij", change, keys[:, segment], precision=highest)
    return (jnp.stack(readouts, axis=1), state)


def body(hidden_in, w_query, w_key, w_value, w_beta, w_out, mem_pos, memory_in):
    seq_count, row_count, local_width = hidden_in.shape
    seg_rows = row_count // SEGS
    mem_count = mem_pos.shape[2]
    local_heads = w_beta.shape[1]
    local_features = w_query.shape[1]
    head_size = local_features // local_heads
    x_float = hidden_in.astype(jnp.float32)
    whole = lax.all_gather(hidden_in, "head", axis=2, tiled=True)
    whole_float = whole.astype(jnp.float32)
    mean_square = jnp.mean(whole_float * whole_float, axis=2, keepdims=True)
    normed = (whole_float * lax.rsqrt(mean_square + epsilon)).astype(jnp.bfloat16)
    full_width = normed.shape[2]
    offsets = (jnp.arange(SEGS, dtype=jnp.int32) * seg_rows)[None, :, None]
    picked = (mem_pos + offsets).reshape(seq_count, SEGS * mem_count)
    memory_rows = jax.vmap(lambda block, where: jnp.take(block, where, axis=0))(normed, picked)
    memory_rows = memory_rows.reshape(seq_count * SEGS * mem_count, full_width)
    token_rows = normed.reshape(seq_count * row_count, full_width)
    piece_query = lax.all_gather(w_query, "batch", axis=0, tiled=True)
    piece_key = lax.all_gather(w_key, "batch", axis=0, tiled=True)
    piece_value = lax.all_gather(w_value, "batch", axis=0, tiled=True)
    piece_beta = lax.all_gather(w_beta, "batch", axis=0, tiled=True)
    query = jnp.dot(token_rows, piece_query, preferred_element_type=jnp.float32)
    keys = jnp.dot(memory_rows, piece_key, preferred_element_type=jnp.float32)
    values = jnp.dot(memory_rows, piece_value, preferred_element_type=jnp.float32)
    logits = jnp.dot(memory_rows, piece_beta, preferred_element_type=jnp.float32)
    query = (query * head_size ** (-0.5)).reshape(seq_count, SEGS, seg_rows, local_heads, head_size)
    keys = keys.reshape(seq_count, SEGS, mem_count, local_heads, head_size)
    keys = keys * lax.rsqrt(jnp.sum(keys * keys, axis=-1, keepdims=True) + 1e-06)
    values = values.reshape(seq_count, SEGS, mem_count, local_heads, head_size)
    beta = jax.nn.sigmoid(logits).reshape(seq_count, SEGS, mem_count, local_heads)
    readout, state = recur(query, keys, values, beta, memory_in)
    readout = readout.reshape(seq_count * row_count, local_features)
    terms = jnp.dot(
        readout,
        lax.all_gather(w_out, "batch", axis=1, tiled=True),
        preferred_element_type=jnp.float32,
    )
    mixed = lax.psum_scatter(terms, "head", scatter_dimension=1, tiled=True)
    hidden_out = (mixed + x_float.reshape(seq_count * row_count, local_width)).astype(jnp.bfloat16)
    return (hidden_out.reshape(hidden_in.shape), state)


def solution(mesh):
    in_specs = (
        P("batch", None, "head"),
        P("batch", "head"),
        P("batch", "head"),
        P("batch", "head"),
        P("batch", "head"),
        P("head", "batch"),
        P("batch", None, None),
        P("batch", "head", None, None),
    )
    out_specs = (P("batch", None, "head"), P("batch", "head", None, None))
    return jax.shard_map(body, mesh=mesh, in_specs=in_specs, out_specs=out_specs, check_vma=False)
```

profile of v0, /device:TPU:0, one launch (start us, length us, event | category | flops | bytes accessed | tf_op | source)
XLA Modules:
  0.0 445.6 jit_solution(10736198151364103323)
XLA Ops:
  7.2 0.0 all-gather.6.cloned.1.call-start
  7.2 0.7 all-gather.6.cloned.1.call-update
  7.9 0.0 all-gather.12.cloned.1.call-start
  7.9 0.7 all-gather.12.cloned.1.call-update
  8.6 0.0 all-gather.10.cloned.1.call-start
  8.7 0.7 all-gather.10.cloned.1.call-update
  9.4 0.0 all-gather.8.cloned.1.call-start
  9.4 0.5 all-gather.8.cloned.1.call-update
  10.0 0.0 all-gather.14.cloned.1.call-start
  10.0 0.5 all-gather.14.cloned.1.call-update
  10.5 0.0 reduce-scatter.2.cloned.1.call-start
  10.6 0.8 broadcast_add_fusion
  11.4 0.1 reshape.261
  11.4 0.1 reshape.260
  11.5 15.9 %all_gather.20 = bf16[4096,8]{0,1:T(8,128)(2,1)S(1)} all-gather(bf16[512,8]{0,1:T(8,128)(2,1)} %param.12), channel_id=1, replica_groups=mesh['head'=4,'batch'=8] {'batch'}, dimensions={0}, use_global_device_ids=true | all-gather | bytes 73728 | tf_op jit(solution)/shard_map/all_gather | solution.py:46
  27.4 20.3 %all-gather.6.cloned.1.call-done = bf16[1,256,4096]{2,1,0:T(8,128)(2,1)} async-done(((bf16[1,256,1024]{2,1,0:T(8,128)(2,1)}), bf16[1,256,4096]{2,1,0:T(8,128)(2,1)}) %all-gather.6.cloned.1.call-update) | async-done | bytes 2097168 | tf_op jit(solution)/shard_map/all_gather | solution.py:33
  47.8 2.1 fusion
  49.8 2.2 fusion.1
  52.0 3.7 gather_fusion
  55.8 0.4 fusion.22
  56.2 0.1 reshape.262
  56.3 1.2 bitcast_select_fusion
  57.5 73.9 %all-gather.12.cloned.1.call-done = bf16[4096,1024]{1,0:T(8,128)(2,1)} async-done(((bf16[512,1024]{1,0:T(8,128)(2,1)}), bf16[4096,1024]{1,0:T(8,128)(2,1)}) %all-gather.12.cloned.1.call-update) | async-done | bytes 8388624 | tf_op jit(solution)/shard_map/all_gather | solution.py:44
  131.4 4.7 %convolution_bitcast_fusion.2 = f32[16,8,8,128]{3,1,2,0:T(8,128)S(1)} fusion(bf16[4096,1024]{1,0:T(8,128)(2,1)} %all-gather.12.cloned.1.call-done, bf16[128,4096]{1,0:T(8,128)(2,1)S(1)} %gather_fusion, pred[128]{0:T(512)(128)(4,1)S(1)} %compare_and_fusion), kind=kOutput, calls=%fused_computation.11 | convolution fusion | flops 1074266112 | bytes 9961600 | tf_op jit(solution)/shard_map/dot_general | solution.py:48
  136.1 0.1 copy.35
  136.2 0.2 multiply_reduce_fusion
  136.4 0.1 copy.28
  136.5 77.1 %all-gather.10.cloned.1.call-done = bf16[4096,1024]{1,0:T(8,128)(2,1)} async-done(((bf16[512,1024]{1,0:T(8,128)(2,1)}), bf16[4096,1024]{1,0:T(8,128)(2,1)}) %all-gather.10.cloned.1.call-update) | async-done | bytes 8388624 | tf_op jit(solution)/shard_map/all_gather | solution.py:45
  213.6 12.1 %copy.27 = bf16[1024,4096]{1,0:T(8,128)(2,1)} copy(bf16[1024,4096]{0,1:T(8,128)(2,1)} %bitcast.131) | data formatting | bytes 16777216 | tf_op jit(solution)/shard_map/dot_general | solution.py:49
  225.7 0.0 copy-start.1
  225.7 69.9 %all-gather.8.cloned.1.call-done = bf16[4096,1024]{1,0:T(8,128)(2,1)} async-done(((bf16[512,1024]{1,0:T(8,128)(2,1)}), bf16[4096,1024]{1,0:T(8,128)(2,1)}) %all-gather.8.cloned.1.call-update) | async-done | bytes 8388624 | tf_op jit(solution)/shard_map/all_gather | solution.py:43
  295.6 0.0 copy-start
  295.6 0.0 copy-start.2
  295.6 5.9 %fusion.7 = f32[32,8,8,128]{3,1,2,0:T(8,128)S(1)} fusion(bf16[4096,1024]{1,0:T(8,128)(2,1)} %all-gather.8.cloned.1.call-done, bf16[1,256,4096]{2,1,0:T(8,128)(2,1)S(1)} %fusion.1), kind=kOutput, calls=%fused_computation.8 | convolution fusion | flops 2147745792 | bytes 11534336 | tf_op jit(solution)/shard_map/dot_general | solution.py:47
  301.5 0.2 copy.34
  301.7 0.1 fusion.34
  301.7 0.0 copy-done.1
  301.7 1.2 fusion.12
  303.0 0.2 copy_multiply_fusion
  303.2 0.0 copy-done
  303.2 0.0 copy-done.2
  303.2 2.9 convolution_bitcast_fusion.3
  306.1 1.1 fusion.17
  307.2 1.0 fusion.10
  308.3 1.2 fusion.13
  309.5 0.1 pad_maximum_fusion
  309.6 0.3 copy.30
  309.9 67.7 %all-gather.14.cloned.1.call-done = bf16[1024,4096]{1,0:T(8,128)(2,1)} async-done(((bf16[1024,512]{1,0:T(8,128)(2,1)}), bf16[1024,4096]{1,0:T(8,128)(2,1)}) %all-gather.14.cloned.1.call-update) | async-done | bytes 8388624 | tf_op jit(solution)/shard_map/all_gather | solution.py:60
  377.6 0.0 copy-start.3
  377.6 7.7 %fusion.25 = f32[256,4096]{1,0:T(8,128)} fusion(bf16[1024,4096]{1,0:T(8,128)(2,1)} %all-gather.14.cloned.1.call-done, bf16[32,8,8,128]{3,2,1,0:T(8,128)(2,1)S(1)} %bitcast.136), kind=kOutput, calls=%fused_computation.36 | convolution fusion | flops 2147483648 | bytes 13107200 | tf_op jit(solution)/shard_map/dot_general | solution.py:58
  385.3 0.0 reduce-scatter.2.cloned.1.call-update
  385.4 1.1 fusion.19
  386.5 1.8 fusion.11
  388.3 48.3 %reduce-scatter.2.cloned.1.call-done = f32[256,1024]{1,0:T(8,128)} async-done(((f32[256,4096]{1,0:T(8,128)}), f32[256,1024]{1,0:T(8,128)}) %reduce-scatter.2.cloned.1.call-update) | async-done | bytes 1048592 | tf_op jit(solution)/shard_map/reduce_scatter | solution.py:63
  436.6 0.0 copy-done.3
  436.6 2.2 fusion.24
  (8 shorter events, 0.1 us)
Async XLA Ops:
  7.2 40.6 %all-gather.6.cloned.1.call-start = ((), (), s32[]{:S(2)}) async-start(), calls=%async_computation.1 | async-start | bytes 2621440 | tf_op jit(solution)/shard_map/all_gather | solution.py:33
  7.9 123.5 %all-gather.12.cloned.1.call-start = ((), (), s32[]{:S(2)}) async-start(), calls=%async_computation.4 | async-start | bytes 9437184 | tf_op jit(solution)/shard_map/all_gather | solution.py:44
  8.6 204.9 %all-gather.10.cloned.1.call-start = ((), (), s32[]{:S(2)}) async-start(), calls=%async_computation.3 | async-start | bytes 9437184 | tf_op jit(solution)/shard_map/all_gather | solution.py:45
  9.4 286.2 %all-gather.8.cloned.1.call-start = ((), (), s32[]{:S(2)}) async-start(), calls=%async_computation.2 | async-start | bytes 9437184 | tf_op jit(solution)/shard_map/all_gather | solution.py:43
  10.0 367.6 %all-gather.14.cloned.1.call-start = ((), (), s32[]{:S(2)}) async-start(), calls=%async_computation.5 | async-start | bytes 9437184 | tf_op jit(solution)/shard_map/all_gather | solution.py:60
  10.5 426.0 %reduce-scatter.2.cloned.1.call-start = ((), (), s32[]{:S(2)}) async-start(), calls=%async_computation.6 | async-start | bytes 5242880 | tf_op jit(solution)/shard_map/reduce_scatter | solution.py:63
  225.7 76.1 %copy-start.1 = (f32[1,8,128,128]{3,2,1,0:T(8,128)S(1)}, f32[1,8,128,128]{3,2,1,0:T(8,128)}, u32[]{:S(2)}) copy-start(f32[1,8,128,128]{3,2,1,0:T(8,128)} %param.15) | copy-start | bytes 1572868
  295.6 7.6 %copy-start = (bf16[1024,4096]{1,0:T(8,128)(2,1)S(1)}, bf16[1024,4096]{1,0:T(8,128)(2,1)}, u32[]{:S(2)}) copy-start(bf16[1024,4096]{1,0:T(8,128)(2,1)} %copy.27) | copy-start | bytes 25165828
  295.6 7.6 %copy-start.2 = (bf16[1,128,1,1,1,1,4096]{6,1,5,4,3,2,0:T(8,128)(2,1)S(1)}, bf16[1,128,1,1,1,1,4096]{6,1,5,4,3,2,0:T(8,128)(2,1)}, u32[]{:S(2)}) copy-start(bf16[1,128,1,1,1,1,4096]{6,1,5,4,3,2,0:T(8,128)(2,1)} %bitcast_select_fusion) | copy-start | bytes 3145732
  377.6 59.0 %copy-start.3 = (bf16[1,256,1024]{2,1,0:T(8,128)(2,1)S(1)}, bf16[1,256,1024]{2,1,0:T(8,128)(2,1)}, u32[]{:S(2)}) copy-start(bf16[1,256,1024]{2,1,0:T(8,128)(2,1)} %param.8) | copy-start | bytes 1572868
Sparse Core Ops, SparseCore 0:
  9.8 37.8 all-gather.5
  49.3 82.0 all-gather.11
  133.0 80.5 all-gather.9
  215.0 80.5 all-gather.7
  297.0 80.5 all-gather.13
  385.5 51.0 reduce-scatter.1
where the time goes:
time: 446 us
  waiting for transfers between devices  360 us (81%)
  matrix products  29.1 us (7%)
  local copies, waits for them, and re-layouts  16.9 us (4%)
  blocking collectives  15.9 us (4%)
  between operations  14.3 us (3%)
  other arithmetic  8.83 us (2%)
    all_gather x1, waiting for transfers between devices, body(): piece_value = lax.all_gather(w_value, 'batch', axis=0, tiled=True)  77.1 us
    all_gather x1, waiting for transfers between devices, body(): piece_key = lax.all_gather(w_key, 'batch', axis=0, tiled=True)  73.9 us
    all_gather x1, waiting for transfers between devices, body(): piece_query = lax.all_gather(w_query, 'batch', axis=0, tiled=True)  69.9 us
    all_gather x1, waiting for transfers between devices, body(): lax.all_gather(w_out, 'batch', axis=1, tiled=True)  67.7 us
    reduce_scatter x1, waiting for transfers between devices, body(): mixed = lax.psum_scatter(terms, 'head', scatter_dimension=1, tiled=True)  48.3 us
    all_gather x1, waiting for transfers between devices, body(): whole = lax.all_gather(hidden_in, 'head', axis=2, tiled=True)  20.3 us
    all_gather x1, blocking collectives, body(): piece_beta = lax.all_gather(w_beta, 'batch', axis=0, tiled=True)  15.9 us
    dot_general x1, local copies, waits for them, and re-layouts, body(): jnp.dot(memory_rows, piece_value, preferred_element_type=jnp.float32)  12.1 us
  transfers between devices with their start and end apart: 6, of which 6 were waited for; matrix products, arithmetic and copies ran while one was open for 10% of the time, Pallas kernels for 0%

commit v1 on v0

--- a/solution.py
+++ b/solution.py
@@ -40,7 +40,8 @@
     memory_rows = jax.vmap(lambda block, where: jnp.take(block, where, axis=0))(normed, picked)
     memory_rows = memory_rows.reshape(seq_count * SEGS * mem_count, full_width)
     token_rows = normed.reshape(seq_count * row_count, full_width)
-    piece_query = lax.all_gather(w_query, "batch", axis=0, tiled=True)
+    stack = jnp.stack([w_query] * lax.axis_size("batch"))
+    piece_query = jnp.concatenate(lax.all_to_all(stack, "batch", 0, 0), axis=0)
     piece_key = lax.all_gather(w_key, "batch", axis=0, tiled=True)
     piece_value = lax.all_gather(w_value, "batch", axis=0, tiled=True)
     piece_beta = lax.all_gather(w_beta, "batch", axis=0, tiled=True)

time: 446 us -> 494 us (1.11)
  blocking collectives: 15.9 us -> 320 us
  waiting for transfers between devices: 360 us -> 93 us
  starting transfers between devices: 0.23 us -> 6.67 us
    all_gather x1, blocking collectives: 15.9 us -> 320 us  [body(): piece_beta = lax.all_gather(w_beta, 'batch', axis=0, tiled=True)]
    all_gather x1, waiting for transfers between devices: 77.1 us -> 0.01 us  [body(): piece_value = lax.all_gather(w_value, 'batch', axis=0, tiled=True)]
    all_gather x1, waiting for transfers between devices: 73.9 us -> 0.01 us  [body(): piece_key = lax.all_gather(w_key, 'batch', axis=0, tiled=True)]
    all_gather x1 -> x0, waiting for transfers between devices: 69.9 us -> none  [body(): piece_query = lax.all_gather(w_query, 'batch', axis=0, tiled=True)]
    all_gather x1, waiting for transfers between devices: 67.7 us -> 42.1 us  [body(): lax.all_gather(w_out, 'batch', axis=1, tiled=True)]
    all_gather x1, waiting for transfers between devices: 20.3 us -> 0.02 us  [body(): whole = lax.all_gather(hidden_in, 'head', axis=2, tiled=True)]
    all_to_all x0 -> x1, starting transfers between devices: none -> 6.49 us  [body(): piece_query = jnp.concatenate(lax.all_to_all(stack, 'batch', 0, 0), axis=0)]
    another operation x0 -> x1, local copies, waits for them, and re-layouts: none -> 5.54 us  [body(): stack = jnp.stack([w_query] * lax.axis_size('batch'))]
  transfers between devices with their start and end apart: 6 -> 6, of which waited for: 6 -> 2; matrix products, arithmetic and copies ran while one was open for 10% -> 10% of each run, Pallas kernels for 0% -> 0%
where the time goes in v1:
time: 494 us; the launch traced here: 493 us
  blocking collectives  320 us (65%)
  waiting for transfers between devices  93 us (19%)
  matrix products  29.9 us (6%)
  local copies, waits for them, and re-layouts  21.6 us (4%)
  between operations  14 us (3%)
  other arithmetic  8.13 us (2%)
  starting transfers between devices  6.67 us (1%)
    all_gather x1, blocking collectives, body(): piece_beta = lax.all_gather(w_beta, 'batch', axis=0, tiled=True)  320 us
    reduce_scatter x1, waiting for transfers between devices, body(): mixed = lax.psum_scatter(terms, 'head', scatter_dimension=1, tiled=True)  48.3 us
    all_gather x1, waiting for transfers between devices, body(): lax.all_gather(w_out, 'batch', axis=1, tiled=True)  42.1 us
    dot_general x1, local copies, waits for them, and re-layouts, body(): jnp.dot(memory_rows, piece_value, preferred_element_type=jnp.float32)  11.2 us
  transfers between devices with their start and end apart: 6, of which 2 were waited for; matrix products, arithmetic and copies ran while one was open for 10% of the time, Pallas kernels for 0%

profile of v1, /device:TPU:0, one launch (start us, length us, event | category | flops | bytes accessed | tf_op | source)
XLA Modules:
  0.0 493.0 jit_solution(12469135170158348019)
XLA Ops:
  7.2 0.0 all-gather.5.cloned.1.call-start
  7.2 0.7 all-gather.5.cloned.1.call-update
  7.9 0.0 all-gather.9.cloned.1.call-start
  7.9 0.7 all-gather.9.cloned.1.call-update
  8.6 0.0 all-gather.7.cloned.1.call-start
  8.7 0.7 all-gather.7.cloned.1.call-update
  9.4 5.5 %stack.8 = bf16[8,512,1024]{2,1,0:T(8,128)(2,1)} broadcast(bf16[512,1024]{1,0:T(8,128)(2,1)} %param.9), dimensions={1,2} | broadcast | bytes 9437184 | tf_op jit(solution)/shard_map/stack | solution.py:43
  14.9 0.0 copy-start.5
  14.9 0.0 copy-start.4
  14.9 6.5 %all-to-all-start = ((bf16[8,512,1024]{2,1,0:T(8,128)(2,1)}), bf16[8,512,1024]{2,1,0:T(8,128)(2,1)}, u32[]{:S(2)}, u32[]{:S(2)}) async-start(bf16[8,512,1024]{2,1,0:T(8,128)(2,1)} %stack.8), calls=%async_computation | async-start | bytes 16777216 | tf_op jit(solution)/shard_map/all_to_all | solution.py:44
  21.4 0.0 all-gather.11.cloned.1.call-start
  21.5 0.5 all-gather.11.cloned.1.call-update
  22.0 0.0 reduce-scatter.2.cloned.1.call-start
  22.0 0.0 copy-done.5
  22.1 0.1 broadcast_add_fusion
  22.1 0.1 reshape.267
  22.2 0.1 reshape.266
  22.3 0.0 copy-done.4
  22.3 319.7 %all_gather.16 = bf16[4096,8]{0,1:T(8,128)(2,1)S(1)} all-gather(bf16[512,8]{0,1:T(8,128)(2,1)S(1)} %copy-done.4), channel_id=1, replica_groups=mesh['head'=4,'batch'=8] {'batch'}, dimensions={0}, use_global_device_ids=true | all-gather | bytes 73728 | tf_op jit(solution)/shard_map/all_gather | solution.py:47
  342.1 0.0 all-gather.5.cloned.1.call-done
  342.1 2.1 fusion
  344.2 2.2 fusion.1
  346.4 3.7 gather_fusion
  350.1 0.4 fusion.22
  350.6 0.1 reshape.268
  350.7 1.1 bitcast_select_fusion
  351.8 0.0 all-gather.9.cloned.1.call-done
  351.8 5.3 %convolution_bitcast_fusion.2 = f32[16,8,8,128]{3,1,2,0:T(8,128)S(1)} fusion(bf16[4096,1024]{1,0:T(8,128)(2,1)} %all-gather.9.cloned.1.call-done, bf16[128,4096]{1,0:T(8,128)(2,1)S(1)} %gather_fusion, pred[128]{0:T(512)(128)(4,1)S(1)} %compare_and_fusion), kind=kOutput, calls=%fused_computation.11 | convolution fusion | flops 1074266112 | bytes 9961600 | tf_op jit(solution)/shard_map/dot_general | solution.py:49
  357.1 0.1 copy.35
  357.2 0.2 multiply_reduce_fusion
  357.5 0.1 copy.28
  357.5 0.0 all-gather.7.cloned.1.call-done
  357.5 11.2 %copy.27 = bf16[1024,4096]{1,0:T(8,128)(2,1)} copy(bf16[1024,4096]{0,1:T(8,128)(2,1)} %bitcast.132) | data formatting | bytes 16777216 | tf_op jit(solution)/shard_map/dot_general | solution.py:50
  368.8 0.0 all-to-all-done
  368.8 0.0 copy-start.1
  368.8 0.0 copy-start
  368.8 0.0 copy-start.2
  368.8 6.0 %fusion.7 = f32[32,8,8,128]{3,1,2,0:T(8,128)S(1)} fusion(bf16[4096,1024]{1,0:T(8,128)(2,1)} %bitcast.1, bf16[1,256,4096]{2,1,0:T(8,128)(2,1)S(1)} %fusion.1), kind=kOutput, calls=%fused_computation.8 | convolution fusion | flops 2147745792 | bytes 11534336 | tf_op jit(solution)/shard_map/dot_general | solution.py:48
  374.7 0.2 copy.34
  375.0 0.1 fusion.34
  375.0 0.0 copy-done.1
  375.0 1.3 fusion.12
  376.3 0.2 copy_multiply_fusion
  376.5 0.0 copy-done
  376.5 0.0 copy-done.2
  376.5 2.9 convolution_bitcast_fusion.3
  379.4 1.1 fusion.17
  380.6 1.0 fusion.10
  381.6 1.3 fusion.13
  382.8 0.1 pad_maximum_fusion
  382.9 0.3 copy.30
  383.2 42.1 %all-gather.11.cloned.1.call-done = bf16[1024,4096]{1,0:T(8,128)(2,1)} async-done(((bf16[1024,512]{1,0:T(8,128)(2,1)}), bf16[1024,4096]{1,0:T(8,128)(2,1)}) %all-gather.11.cloned.1.call-update) | async-done | bytes 8388624 | tf_op jit(solution)/shard_map/all_gather | solution.py:61
  425.3 0.0 copy-start.3
  425.3 7.7 %fusion.25 = f32[256,4096]{1,0:T(8,128)} fusion(bf16[1024,4096]{1,0:T(8,128)(2,1)} %all-gather.11.cloned.1.call-done, bf16[32,8,8,128]{3,2,1,0:T(8,128)(2,1)S(1)} %bitcast.137), kind=kOutput, calls=%fused_computation.36 | convolution fusion | flops 2147483648 | bytes 13107200 | tf_op jit(solution)/shard_map/dot_general | solution.py:59
  433.0 0.0 reduce-scatter.2.cloned.1.call-update
  433.1 1.1 fusion.19
  434.2 1.8 fusion.11
  436.0 48.3 %reduce-scatter.2.cloned.1.call-done = f32[256,1024]{1,0:T(8,128)} async-done(((f32[256,4096]{1,0:T(8,128)}), f32[256,1024]{1,0:T(8,128)}) %reduce-scatter.2.cloned.1.call-update) | async-done | bytes 1048592 | tf_op jit(solution)/shard_map/reduce_scatter | solution.py:64
  484.3 0.0 copy-done.3
  484.3 2.2 fusion.24
  (8 shorter events, 0.1 us)
Async XLA Ops:
  7.2 334.9 %all-gather.5.cloned.1.call-start = ((), (), s32[]{:S(2)}) async-start(), calls=%async_computation.2 | async-start | bytes 2621440 | tf_op jit(solution)/shard_map/all_gather | solution.py:33
  7.9 343.9 %all-gather.9.cloned.1.call-start = ((), (), s32[]{:S(2)}) async-start(), calls=%async_computation.4 | async-start | bytes 9437184 | tf_op jit(solution)/shard_map/all_gather | solution.py:45
  8.6 348.9 %all-gather.7.cloned.1.call-start = ((), (), s32[]{:S(2)}) async-start(), calls=%async_computation.3 | async-start | bytes 9437184 | tf_op jit(solution)/shard_map/all_gather | solution.py:46
  14.9 7.1 %copy-start.5 = (s32[1,2,64]{2,1,0:T(2,128)S(1)}, s32[1,2,64]{2,1,0:T(2,128)}, u32[]{:S(2)}) copy-start(s32[1,2,64]{2,1,0:T(2,128)} %param.14) | copy-start | bytes 1540
  14.9 7.4 %copy-start.4 = (bf16[512,8]{0,1:T(8,128)(2,1)S(1)}, bf16[512,8]{0,1:T(8,128)(2,1)}, u32[]{:S(2)}) copy-start(bf16[512,8]{0,1:T(8,128)(2,1)} %param.12) | copy-start | bytes 24580
  14.9 353.8 %all-to-all-start = ((bf16[8,512,1024]{2,1,0:T(8,128)(2,1)}), bf16[8,512,1024]{2,1,0:T(8,128)(2,1)}, u32[]{:S(2)}, u32[]{:S(2)}) async-start(bf16[8,512,1024]{2,1,0:T(8,128)(2,1)} %stack.8), calls=%async_computation | async-start | bytes 16777216 | tf_op jit(solution)/shard_map/all_to_all | solution.py:44
  21.4 403.9 %all-gather.11.cloned.1.call-start = ((), (), s32[]{:S(2)}) async-start(), calls=%async_computation.5 | async-start | bytes 9437184 | tf_op jit(solution)/shard_map/all_gather | solution.py:61
  22.0 462.3 %reduce-scatter.2.cloned.1.call-start = ((), (), s32[]{:S(2)}) async-start(), calls=%async_computation.6 | async-start | bytes 5242880 | tf_op jit(solution)/shard_map/reduce_scatter | solution.py:64
  368.8 6.3 %copy-start.1 = (f32[1,8,128,128]{3,2,1,0:T(8,128)S(1)}, f32[1,8,128,128]{3,2,1,0:T(8,128)}, u32[]{:S(2)}) copy-start(f32[1,8,128,128]{3,2,1,0:T(8,128)} %param.15) | copy-start | bytes 1572868
  368.8 7.8 %copy-start = (bf16[1024,4096]{1,0:T(8,128)(2,1)S(1)}, bf16[1024,4096]{1,0:T(8,128)(2,1)}, u32[]{:S(2)}) copy-start(bf16[1024,4096]{1,0:T(8,128)(2,1)} %copy.27) | copy-start | bytes 25165828
  368.8 7.8 %copy-start.2 = (bf16[1,128,1,1,1,1,4096]{6,1,5,4,3,2,0:T(8,128)(2,1)S(1)}, bf16[1,128,1,1,1,1,4096]{6,1,5,4,3,2,0:T(8,128)(2,1)}, u32[]{:S(2)}) copy-start(bf16[1,128,1,1,1,1,4096]{6,1,5,4,3,2,0:T(8,128)(2,1)} %bitcast_select_fusion) | copy-start | bytes 3145732
  425.3 59.0 %copy-start.3 = (bf16[1,256,1024]{2,1,0:T(8,128)(2,1)S(1)}, bf16[1,256,1024]{2,1,0:T(8,128)(2,1)}, u32[]{:S(2)}) copy-start(bf16[1,256,1024]{2,1,0:T(8,128)(2,1)} %param.8) | copy-start | bytes 1572868
Sparse Core Ops, SparseCore 0:
  9.8 37.8 all-gather.4
  49.4 187.8 all-gather.8
  238.8 103.8 all-gather.6
  344.2 81.0 all-gather.10
  433.2 51.0 reduce-scatter.1
